TPU v7x, 32 devices: a whole 2x2x4 slice. The times are simulated.
32 devices in a mesh: dp: 8 (over y, x, core), fsdp: 4 (over z).
Axes of the slice: x: 2, y: 2, z: 4, core: 2. Of those that a mesh axis runs over, the one named last changes fastest.
Arguments:
- gene_ids: int32 [32, 2048], P(('dp', 'fsdp')), may hold values from 0 to 12799
- expr_bins: int32 [32, 2048], P(('dp', 'fsdp')), may hold values from 0 to 63
- study_ids: int32 [32], P(('dp', 'fsdp')), may hold values from 0 to 63
- lengths: int32 [32], P(('dp', 'fsdp')), may hold values from 256 to 2048, as said below
- prior_embed: bfloat16 [32, 2048, 256], P(('dp', 'fsdp')), may hold values from -3 to 3
- cotangent: bfloat16 [32, 2048, 256], P(('dp', 'fsdp')), may hold values from -6 to 6
- gene_table: bfloat16 [12800, 256], P('fsdp'), may hold values from -3 to 3
- expr_table: bfloat16 [64, 256], P('fsdp'), may hold values from -3 to 3
- study_table: bfloat16 [64, 256], P('fsdp'), may hold values from -3 to 3
- position_table: bfloat16 [2048, 256], P('fsdp'), may hold values from -3 to 3
- norm1_gain: bfloat16 [256], P('fsdp'), may hold values from 0.099609375 to 1.8984375
- norm1_shift: bfloat16 [256], P('fsdp'), may hold values from -1.5 to 1.5
- w_qkv: bfloat16 [256, 768], P('fsdp'), may hold values from -0.375 to 0.375
- bias_query: bfloat16 [256], P('fsdp'), may hold values from -1.5 to 1.5
- bias_value: bfloat16 [256], P('fsdp'), may hold values from -1.5 to 1.5
- w_output: bfloat16 [256, 256], P('fsdp'), may hold values from -6 to 6
- bias_output: bfloat16 [256], P('fsdp'), may hold values from -1.5 to 1.5
- norm2_gain: bfloat16 [256], P('fsdp'), may hold values from 0.099609375 to 1.8984375
- norm2_shift: bfloat16 [256], P('fsdp'), may hold values from -1.5 to 1.5
- w_up_proj: bfloat16 [256, 512], P('fsdp'), may hold values from -0.375 to 0.375
- bias_up: bfloat16 [512], P('fsdp'), may hold values from -1.5 to 1.5
- w_down_proj: bfloat16 [512, 256], P('fsdp'), may hold values from -0.25 to 0.25
- bias_down: bfloat16 [256], P('fsdp'), may hold values from -1.5 to 1.5
Outputs:
- hidden_out: bfloat16 [32, 2048, 256], P(('dp', 'fsdp'))
- grad_gene_table: float32 [12800, 256], P('fsdp')
- update_count: int32 [12800], P('fsdp')
- grad_expr_table: float32 [64, 256], P('fsdp')
- grad_study_table: float32 [64, 256], P('fsdp')
- grad_position_table: float32 [2048, 256], P('fsdp')
- grad_norm1_gain: float32 [256], P('fsdp')
- grad_norm1_shift: float32 [256], P('fsdp')
- grad_w_qkv: float32 [256, 768], P('fsdp')
- grad_bias_query: float32 [256], P('fsdp')
- grad_bias_value: float32 [256], P('fsdp')
- grad_w_output: float32 [256, 256], P('fsdp')
- grad_bias_output: float32 [256], P('fsdp')
- grad_norm2_gain: float32 [256], P('fsdp')
- grad_norm2_shift: float32 [256], P('fsdp')
- grad_w_up_proj: float32 [256, 512], P('fsdp')
- grad_bias_up: float32 [512], P('fsdp')
- grad_w_down_proj: float32 [512, 256], P('fsdp')
- grad_bias_down: float32 [256], P('fsdp')
Inputs may be any that keep to these rules, and one draw needn't show every extreme that they name: Slots from lengths[c] on are padding; some cell has 2048 genes and some 2048 // 8.
All inputs are finite; a program needn't handle non-finite values.
Results may differ from a plain program's by a relative error of at most 0.0082.
Values may be sent and summed in bfloat16 or wider, within the bound.
No kernel may reach another device: no remote copies, remote signals or barrier semaphores. Data moves between devices by JAX's collectives and lax.ppermute only.
A program may use at most 128 MiB of HBM per device.

v0:
```python
import jax
import jax.numpy as jnp
from jax import lax
from jax.sharding import PartitionSpec as P

HEADS = 4
epsilon = 1e-05
highest = lax.Precision.HIGHEST


def normalize(values):
    average = jnp.mean(values, axis=-1, keepdims=True)
    centered = values - average
    variance = jnp.mean(centered * centered, axis=-1, keepdims=True)
    return centered * lax.rsqrt(variance + epsilon)


def norm_back(values, gain, grad):
    unused, pullback = jax.vjp(lambda entries, scale: normalize(entries) * scale, values, gain)
    grad_rows, grad_gain = pullback(grad)
    return (grad_rows, grad_gain, jnp.sum(grad, axis=0))


def matmul(left, right):
    return jnp.dot(left, right, preferred_element_type=jnp.float32)


def weight_grad(left, right):
    return lax.dot_general(
        left, right, (((0,), (0,)), ((), ())), preferred_element_type=jnp.float32
    )


def back_matmul(left, right):
    return lax.dot_general(
        left, right, (((1,), (1,)), ((), ())), preferred_element_type=jnp.float32
    )


def table_grad(hits, grads):
    return lax.dot_general(
        hits, grads, (((0,), (0,)), ((), ())), precision=highest, preferred_element_type=jnp.float32
    )


def attend(query, keys, values, key_mask, block):
    length, heads, head_size = query.shape
    scale = head_size ** (-0.5)
    query_blocks = query.reshape(length // block, block, heads, head_size)

    def one_block(query_block):
        scores = (
            jnp.einsum("qhk,shk->hqs", query_block, keys, preferred_element_type=jnp.float32)
            * scale
        )
        scores = jnp.where(key_mask[None, None, :] > 0, scores, -1000000000.0)
        peak = jnp.max(scores, axis=-1, keepdims=True)
        raised = jnp.exp(scores - peak)
        total = jnp.sum(raised, axis=-1, keepdims=True)
        probs = (raised / total).astype(jnp.bfloat16)
        attended = jnp.einsum("hqs,shk->qhk", probs, values, preferred_element_type=jnp.float32)
        return (attended.astype(jnp.bfloat16), (peak + jnp.log(total))[..., 0])

    attended, log_total = lax.map(one_block, query_blocks)
    return (attended.reshape(length, heads, head_size), log_total)


def attend_back(query, keys, values, key_mask, log_total, grad_attended, block):
    length, heads, head_size = query.shape
    scale = head_size ** (-0.5)
    query_blocks = query.reshape(length // block, block, heads, head_size)
    grad_blocks = grad_attended.reshape(length // block, block, heads, head_size)

    def one_block(carry, embedding_parts):
        grad_keys, grad_values = carry
        query_block, grad_block, log_block = embedding_parts
        scores = (
            jnp.einsum("qhk,shk->hqs", query_block, keys, preferred_element_type=jnp.float32)
            * scale
        )
        scores = jnp.where(key_mask[None, None, :] > 0, scores, -1000000000.0)
        probs = jnp.exp(scores - log_block[..., None])
        probs_low = probs.astype(jnp.bfloat16)
        grad_probs = jnp.einsum(
            "qhk,shk->hqs", grad_block, values, preferred_element_type=jnp.float32
        )
        inner = jnp.sum(probs * grad_probs, axis=-1, keepdims=True)
        grad_scores = (probs * (grad_probs - inner)).astype(jnp.bfloat16)
        grad_query = (
            jnp.einsum("hqs,shk->qhk", grad_scores, keys, preferred_element_type=jnp.float32)
            * scale
        )
        grad_keys = (
            grad_keys
            + jnp.einsum(
                "hqs,qhk->shk", grad_scores, query_block, preferred_element_type=jnp.float32
            )
            * scale
        )
        grad_values = grad_values + jnp.einsum(
            "hqs,qhk->shk", probs_low, grad_block, preferred_element_type=jnp.float32
        )
        return ((grad_keys, grad_values), grad_query)

    starting = jnp.zeros((length, heads, head_size), jnp.float32)
    (grad_keys, grad_values), grad_query = lax.scan(
        one_block, (starting, starting), (query_blocks, grad_blocks, log_total)
    )
    return (grad_query.reshape(length, heads, head_size), grad_keys, grad_values)


def body(
    gene_ids,
    expr_bins,
    study_ids,
    lengths,
    prior_embed,
    cotangent,
    gene_table,
    expr_table,
    study_table,
    position_table,
    norm1_gain,
    norm1_shift,
    w_qkv,
    bias_query,
    bias_value,
    w_output,
    bias_output,
    norm2_gain,
    norm2_shift,
    w_up_proj,
    bias_up,
    w_down_proj,
    bias_down,
):
    (
        full_gene,
        full_expr,
        full_study,
        full_position,
        gain_one,
        shift_one,
        full_qkv,
        query_bias,
        value_bias,
        full_output,
        output_bias,
        gain_two,
        shift_two,
        full_up,
        up_bias,
        full_down,
        down_bias,
    ) = (
        lax.all_gather(gene_table, "fsdp", axis=0, tiled=True),
        lax.all_gather(expr_table, "fsdp", axis=0, tiled=True),
        lax.all_gather(study_table, "fsdp", axis=0, tiled=True),
        lax.all_gather(position_table, "fsdp", axis=0, tiled=True),
        lax.all_gather(norm1_gain, "fsdp", axis=0, tiled=True),
        lax.all_gather(norm1_shift, "fsdp", axis=0, tiled=True),
        lax.all_gather(w_qkv, "fsdp", axis=0, tiled=True),
        lax.all_gather(bias_query, "fsdp", axis=0, tiled=True),
        lax.all_gather(bias_value, "fsdp", axis=0, tiled=True),
        lax.all_gather(w_output, "fsdp", axis=0, tiled=True),
        lax.all_gather(bias_output, "fsdp", axis=0, tiled=True),
        lax.all_gather(norm2_gain, "fsdp", axis=0, tiled=True),
        lax.all_gather(norm2_shift, "fsdp", axis=0, tiled=True),
        lax.all_gather(w_up_proj, "fsdp", axis=0, tiled=True),
        lax.all_gather(bias_up, "fsdp", axis=0, tiled=True),
        lax.all_gather(w_down_proj, "fsdp", axis=0, tiled=True),
        lax.all_gather(bias_down, "fsdp", axis=0, tiled=True),
    )
    cells, length = gene_ids.shape
    width = full_gene.shape[1]
    rows = cells * length
    heads = HEADS
    head_size = width // heads
    block = min(512, length)

    def shaped(array):
        return array.reshape(cells, length, heads, head_size)

    key_mask = (lax.broadcasted_iota(jnp.int32, (cells, length), 1) < lengths[:, None]).astype(
        jnp.float32
    )
    flat_mask = key_mask.reshape(rows, 1)
    embedded = (
        full_gene[gene_ids].astype(jnp.float32)
        + full_expr[expr_bins].astype(jnp.float32)
        + full_study[study_ids].astype(jnp.float32)[:, None, :]
        + full_position.astype(jnp.float32)[None]
        + prior_embed.astype(jnp.float32)
    )
    inputs = (embedded * key_mask[..., None]).reshape(rows, width)
    normed_one = (
        normalize(inputs) * gain_one.astype(jnp.float32) + shift_one.astype(jnp.float32)
    ).astype(jnp.bfloat16)
    mixed = matmul(normed_one, full_qkv)
    query = (mixed[:, :width] + query_bias.astype(jnp.float32)).astype(jnp.bfloat16)
    keys = mixed[:, width : 2 * width].astype(jnp.bfloat16)
    values = (mixed[:, 2 * width :] + value_bias.astype(jnp.float32)).astype(jnp.bfloat16)
    attended, log_total = lax.map(
        lambda embedding_parts: attend(
            embedding_parts[0], embedding_parts[1], embedding_parts[2], embedding_parts[3], block
        ),
        (shaped(query), shaped(keys), shaped(values), key_mask),
    )
    attended = attended.reshape(rows, width)
    branch = matmul(attended, full_output) + output_bias.astype(jnp.float32)
    middle = inputs + branch
    normed_two = (
        normalize(middle) * gain_two.astype(jnp.float32) + shift_two.astype(jnp.float32)
    ).astype(jnp.bfloat16)
    upward = matmul(normed_two, full_up) + up_bias.astype(jnp.float32)
    activated = jax.nn.gelu(upward, approximate=False).astype(jnp.bfloat16)
    result = (middle + (matmul(activated, full_down) + down_bias.astype(jnp.float32))) * flat_mask
    hidden_out = result.astype(jnp.bfloat16).reshape(cells, length, width)
    back_gain_one, back_qkv, back_output, back_gain_two, back_up, back_down = (
        lax.all_gather(norm1_gain, "fsdp", axis=0, tiled=True),
        lax.all_gather(w_qkv, "fsdp", axis=0, tiled=True),
        lax.all_gather(w_output, "fsdp", axis=0, tiled=True),
        lax.all_gather(norm2_gain, "fsdp", axis=0, tiled=True),
        lax.all_gather(w_up_proj, "fsdp", axis=0, tiled=True),
        lax.all_gather(w_down_proj, "fsdp", axis=0, tiled=True),
    )
    grad_result = cotangent.astype(jnp.float32).reshape(rows, width) * flat_mask
    grad_low = grad_result.astype(jnp.bfloat16)
    grad_down_w = weight_grad(activated, grad_low)
    grad_down_b = jnp.sum(grad_result, axis=0)
    grad_activated = back_matmul(grad_low, back_down)
    unused, gelu_pull = jax.vjp(lambda entries: jax.nn.gelu(entries, approximate=False), upward)
    grad_upward = gelu_pull(grad_activated)[0].astype(jnp.bfloat16)
    grad_up_w = weight_grad(normed_two, grad_upward)
    grad_up_b = jnp.sum(grad_upward.astype(jnp.float32), axis=0)
    grad_normed_two = back_matmul(grad_upward, back_up)
    grad_mid_norm, grad_gain_two, grad_shift_two = norm_back(
        middle, back_gain_two.astype(jnp.float32), grad_normed_two
    )
    grad_middle = grad_result + grad_mid_norm
    grad_branch = grad_middle.astype(jnp.bfloat16)
    grad_output_w = weight_grad(attended, grad_branch)
    grad_output_b = jnp.sum(grad_branch.astype(jnp.float32), axis=0)
    grad_attended = back_matmul(grad_branch, back_output).astype(jnp.bfloat16)
    grad_query, grad_keys, grad_values = lax.map(
        lambda embedding_parts: attend_back(
            embedding_parts[0],
            embedding_parts[1],
            embedding_parts[2],
            embedding_parts[3],
            embedding_parts[4],
            embedding_parts[5],
            block,
        ),
        (shaped(query), shaped(keys), shaped(values), key_mask, log_total, shaped(grad_attended)),
    )
    grad_query = grad_query.reshape(rows, width).astype(jnp.bfloat16)
    grad_keys = grad_keys.reshape(rows, width).astype(jnp.bfloat16)
    grad_values = grad_values.reshape(rows, width).astype(jnp.bfloat16)
    grad_mixed = jnp.concatenate([grad_query, grad_keys, grad_values], axis=1)
    grad_qkv_w = weight_grad(normed_one, grad_mixed)
    grad_query_b = jnp.sum(grad_query.astype(jnp.float32), axis=0)
    grad_value_b = jnp.sum(grad_values.astype(jnp.float32), axis=0)
    grad_normed_one = back_matmul(grad_mixed, back_qkv)
    grad_in_norm, grad_gain_one, grad_shift_one = norm_back(
        inputs, back_gain_one.astype(jnp.float32), grad_normed_one
    )
    grad_inputs = (grad_middle + grad_in_norm) * flat_mask
    grad_cells = grad_inputs.reshape(cells, length, width)
    bin_hits = (
        expr_bins.reshape(rows, 1) == lax.broadcasted_iota(jnp.int32, (1, full_expr.shape[0]), 1)
    ).astype(jnp.float32)
    grad_expr = table_grad(bin_hits, grad_inputs)
    study_hits = (
        study_ids[:, None] == lax.broadcasted_iota(jnp.int32, (1, full_study.shape[0]), 1)
    ).astype(jnp.float32)
    grad_study = table_grad(study_hits, jnp.sum(grad_cells, axis=1))
    grad_position = jnp.sum(grad_cells, axis=0)
    flat_ids = gene_ids.reshape(rows)
    vocab = full_gene.shape[0]
    dense_grad = jnp.zeros((vocab, width), jnp.float32).at[flat_ids].add(grad_inputs)
    dense_count = jnp.zeros((vocab,), jnp.float32).at[flat_ids].add(flat_mask[:, 0])
    (
        table_share,
        count_share,
        expr_share,
        study_share,
        position_share,
        gain_one_share,
        shift_one_share,
        qkv_share,
        query_b_share,
        value_b_share,
        output_share,
        output_b_share,
        gain_two_share,
        shift_two_share,
        up_share,
        up_b_share,
        down_share,
        down_b_share,
    ) = (
        lax.psum_scatter(dense_grad, "fsdp", scatter_dimension=0, tiled=True),
        lax.psum_scatter(dense_count, "fsdp", scatter_dimension=0, tiled=True),
        lax.psum_scatter(grad_expr, "fsdp", scatter_dimension=0, tiled=True),
        lax.psum_scatter(grad_study, "fsdp", scatter_dimension=0, tiled=True),
        lax.psum_scatter(grad_position, "fsdp", scatter_dimension=0, tiled=True),
        lax.psum_scatter(grad_gain_one, "fsdp", scatter_dimension=0, tiled=True),
        lax.psum_scatter(grad_shift_one, "fsdp", scatter_dimension=0, tiled=True),
        lax.psum_scatter(grad_qkv_w, "fsdp", scatter_dimension=0, tiled=True),
        lax.psum_scatter(grad_query_b, "fsdp", scatter_dimension=0, tiled=True),
        lax.psum_scatter(grad_value_b, "fsdp", scatter_dimension=0, tiled=True),
        lax.psum_scatter(grad_output_w, "fsdp", scatter_dimension=0, tiled=True),
        lax.psum_scatter(grad_output_b, "fsdp", scatter_dimension=0, tiled=True),
        lax.psum_scatter(grad_gain_two, "fsdp", scatter_dimension=0, tiled=True),
        lax.psum_scatter(grad_shift_two, "fsdp", scatter_dimension=0, tiled=True),
        lax.psum_scatter(grad_up_w, "fsdp", scatter_dimension=0, tiled=True),
        lax.psum_scatter(grad_up_b, "fsdp", scatter_dimension=0, tiled=True),
        lax.psum_scatter(grad_down_w, "fsdp", scatter_dimension=0, tiled=True),
        lax.psum_scatter(grad_down_b, "fsdp", scatter_dimension=0, tiled=True),
    )
    (
        table_sum,
        count_sum,
        expr_sum,
        study_sum,
        position_sum,
        gain_one_sum,
        shift_one_sum,
        qkv_sum,
        query_b_sum,
        value_b_sum,
        output_sum,
        output_b_sum,
        gain_two_sum,
        shift_two_sum,
        up_sum,
        up_b_sum,
        down_sum,
        down_b_sum,
    ) = lax.psum(
        (
            table_share,
            count_share,
            expr_share,
            study_share,
            position_share,
            gain_one_share,
            shift_one_share,
            qkv_share,
            query_b_share,
            value_b_share,
            output_share,
            output_b_share,
            gain_two_share,
            shift_two_share,
            up_share,
            up_b_share,
            down_share,
            down_b_share,
        ),
        "dp",
    )
    return (
        hidden_out,
        table_sum,
        count_sum.astype(jnp.int32),
        expr_sum,
        study_sum,
        position_sum,
        gain_one_sum,
        shift_one_sum,
        qkv_sum,
        query_b_sum,
        value_b_sum,
        output_sum,
        output_b_sum,
        gain_two_sum,
        shift_two_sum,
        up_sum,
        up_b_sum,
        down_sum,
        down_b_sum,
    )


def solution(mesh):
    return jax.shard_map(
        body,
        mesh=mesh,
        in_specs=(
            P(("dp", "fsdp"), None),
            P(("dp", "fsdp"), None),
            P(("dp", "fsdp")),
            P(("dp", "fsdp")),
            P(("dp", "fsdp"), None, None),
            P(("dp", "fsdp"), None, None),
            P("fsdp", None),
            P("fsdp", None),
            P("fsdp", None),
            P("fsdp", None),
            P("fsdp"),
            P("fsdp"),
            P("fsdp", None),
            P("fsdp"),
            P("fsdp"),
            P("fsdp", None),
            P("fsdp"),
            P("fsdp"),
            P("fsdp"),
            P("fsdp", None),
            P("fsdp"),
            P("fsdp", None),
            P("fsdp"),
        ),
        out_specs=(
            P(("dp", "fsdp"), None, None),
            P("fsdp", None),
            P("fsdp"),
            P("fsdp", None),
            P("fsdp", None),
            P("fsdp", None),
            P("fsdp"),
            P("fsdp"),
            P("fsdp", None),
            P("fsdp"),
            P("fsdp"),
            P("fsdp", None),
            P("fsdp"),
            P("fsdp"),
            P("fsdp"),
            P("fsdp", None),
            P("fsdp"),
            P("fsdp", None),
            P("fsdp"),
        ),
        check_vma=False,
    )
```

profile of v0, /device:TPU:0, one launch (start us, length us, event | category | flops | bytes accessed | tf_op | source)
XLA Modules:
  0.0 905.6 jit_solution(10123542352486221909)
XLA Ops:
  20.7 16.2 %all-reduce.21 = (bf16[256]{0:T(256)(128)(2,1)S(1)}, bf16[256]{0:T(256)(128)(2,1)S(1)}, bf16[256]{0:T(256)(128)(2,1)S(1)}, bf16[256]{0:T(256)(128)(2,1)S(1)}, bf...) all-reduce(bf16[256]{0:T(256)(128)(2,1)S(1)} %dynamic-update-slice., ...), channel_id=1, replica_groups=mesh['dp'=8,'fsdp'=4] {'fsdp'}, use_global_device_ids=true, to_apply=%add.1 | all-reduce | flops 2048 | bytes 8192
  40.7 7.9 all-gather
  49.2 16.0 %all_gather.58 = bf16[64,256]{1,0:T(8,128)(2,1)S(1)} all-gather(bf16[16,256]{1,0:T(8,128)(2,1)} %param.34), channel_id=1, replica_groups=mesh['dp'=8,'fsdp'=4] {'fsdp'}, dimensions={0}, use_global_device_ids=true | all-gather | bytes 40960 | tf_op jit(solution)/shard_map/all_gather | solution.py:157
  65.2 7.5 gather_fusion.1
  76.3 15.8 %all_gather.59 = bf16[64,256]{1,0:T(8,128)(2,1)S(1)} all-gather(bf16[16,256]{1,0:T(8,128)(2,1)S(1)} %copy-done.55), channel_id=1, replica_groups=mesh['dp'=8,'fsdp'=4] {'fsdp'}, dimensions={0}, use_global_device_ids=true | all-gather | bytes 40960 | tf_op jit(solution)/shard_map/all_gather | solution.py:158
  92.2 18.9 %all_gather.66 = bf16[256,256]{1,0:T(8,128)(2,1)} all-gather(bf16[64,256]{1,0:T(8,128)(2,1)S(1)} %copy-done.49), channel_id=1, replica_groups=mesh['dp'=8,'fsdp'=4] {'fsdp'}, dimensions={0}, use_global_device_ids=true | all-gather | bytes 163840 | tf_op jit(solution)/shard_map/all_gather | solution.py:165
  111.1 22.1 %all_gather.70 = bf16[256,512]{1,0:T(8,128)(2,1)} all-gather(bf16[64,512]{1,0:T(8,128)(2,1)S(1)} %copy-done.44), channel_id=1, replica_groups=mesh['dp'=8,'fsdp'=4] {'fsdp'}, dimensions={0}, use_global_device_ids=true | all-gather | bytes 327680 | tf_op jit(solution)/shard_map/all_gather | solution.py:169
  133.2 16.9 %all_gather.72 = bf16[512,256]{1,0:T(8,128)(2,1)} all-gather(bf16[128,256]{1,0:T(8,128)(2,1)S(1)} %copy-done.45), channel_id=1, replica_groups=mesh['dp'=8,'fsdp'=4] {'fsdp'}, dimensions={0}, use_global_device_ids=true | all-gather | bytes 327680 | tf_op jit(solution)/shard_map/all_gather | solution.py:171
  150.7 17.1 %all_gather.63 = bf16[256,768]{1,0:T(8,128)(2,1)S(1)} all-gather(bf16[64,768]{1,0:T(8,128)(2,1)} %param.39), channel_id=1, replica_groups=mesh['dp'=8,'fsdp'=4] {'fsdp'}, dimensions={0}, use_global_device_ids=true | all-gather | bytes 491520 | tf_op jit(solution)/shard_map/all_gather | solution.py:162
  167.8 12.3 %gather_fusion = bf16[2048,256]{1,0:T(8,128)(2,1)} fusion(bf16[12800,256]{1,0:T(8,128)(2,1)} %all-gather.4.cloned.1.call-done, s32[2048]{0:T(1024)S(1)} %broadcast_clamp_fusion.1), kind=kCustom, calls=%fused_computation | custom fusion | bytes 2105344 | tf_op jit(solution)/shard_map/gather | solution.py:189
  191.9 53.9 %while.49 = (s32[]{:T(128)}, bf16[4,512,4,64]{1,3,2,0:T(8,128)(2,1)}, f32[4,4,512]{2,1,0:T(4,128)S(1)}, bf16[4,512,4,64]{1,3,2,0:T(8,128)(2,1)}, bf16[2048,4,64]...) while((s32[]{:T(128)}, bf16[4,512,4,64]{1,3,2,0:T(8,128)(2,1)}, ...), condition=%wide.region_5.6_spmd.clone, body=%wide.region_2.5_spmd.clone.sunk | while | flops 1124208640 | bytes 53026924 | solution.py:64
  249.5 10.9 %multiply_convert_fusion.1 = (bf16[2048,512]{1,0:T(8,128)(2,1)}, f32[2048,512]{1,0:T(8,128)S(1)}, f32[2048,512]{1,0:T(8,128)S(1)}) fusion(f32[512]{0:T(512)S(1)} %bitcast.190, bf16[256,512]{1,0:T(8,128)(2,1)S(1)} %copy-done.26, f32[2048,256]{0,1:T(8,128)S(1)} %get-tuple-element.435, f32[256]{0:T(256)S(1)} %copy-done.72, f32[256]{0:T(256)S(1)} %copy-done.64, ...), kind=kOutput, calls=%fused_computation.63 | convolution fusion | flops 608698368 | bytes 12865536 | tf_op jit(solution)/shard_map/dot_general | solution.py:25
  297.0 166.8 %while.50 = (s32[]{:T(128)}, f32[2048,4,64]{0,2,1:T(8,128)}, f32[2048,4,64]{0,2,1:T(8,128)}, bf16[4,512,4,64]{1,3,2,0:T(8,128)(2,1)}, bf16[4,512,4,64]{1,3,2,0:T...) while((s32[]{:T(128)}, f32[2048,4,64]{0,2,1:T(8,128)}, ...), condition=%wide.region_12.13_spmd.clone, body=%wide.region_10.12_spmd.clone.sunk | while | flops 2750025728 | bytes 172556464 | solution.py:106
  306.8 9.5 %multiply_reduce_fusion.8 = (f32[4,512]{1,0:T(4,128)S(1)}, f32[4,512,2048]{2,1,0:T(8,128)}) fusion(f32[4,512,2048]{2,1,0:T(8,128)S(1)} %fusion.154, f32[4,512]{1,0:T(4,128)S(1)} %dynamic-slice_bitcast_fusion.2, pred[2048]{0:T(1024)(128)(4,1)S(1)} %convert_compare_fusion.5, bf16[2048,4,64]{0,2,1:T(8,128)(2,1)S(1)} %get-tuple-element.611, ...), kind=kOutput, calls=%fused_computation.25.clone.1 | convolution fusion | flops 557840384 | bytes 34883588 | tf_op jit(solution)/shard_map/while/body/eval_jaxpr/while/body/eval_jaxpr/qhk,shk->hqs/dot_general | solution.py:84
  316.4 10.8 %multiply_convert_fusion.3 = bf16[4,512,2048]{2,1,0:T(8,128)(2,1)} fusion(f32[4,512,2048]{2,1,0:T(8,128)} %get-tuple-element.553, f32[4,512,2048]{2,1,0:T(8,128)S(1)} %fusion.154, f32[4,512]{1,0:T(4,128)S(1)} %get-tuple-element.554, f32[4,512]{1,0:T(4,128)S(1)} %dynamic-slice_bitcast_fusion.2, pred[2048]{0:T(1024)(128)(4,1)S(1)} %convert_compare_fusion.5), kind=kLoop, calls=%fused_computation.24.clone.1 | loop fusion | flops 25165824 | bytes 41961472 | tf_op jit(solution)/shard_map/while/body/eval_jaxpr/while/body/eval_jaxpr/convert_element_type | solution.py:88
  327.1 6.9 fusion.157
  348.1 9.5 %multiply_reduce_fusion.8 = (f32[4,512]{1,0:T(4,128)S(1)}, f32[4,512,2048]{2,1,0:T(8,128)}) fusion(f32[4,512,2048]{2,1,0:T(8,128)S(1)} %fusion.154, f32[4,512]{1,0:T(4,128)S(1)} %dynamic-slice_bitcast_fusion.2, pred[2048]{0:T(1024)(128)(4,1)S(1)} %convert_compare_fusion.5, bf16[2048,4,64]{0,2,1:T(8,128)(2,1)S(1)} %get-tuple-element.611, ...), kind=kOutput, calls=%fused_computation.25.clone.1 | convolution fusion | flops 557840384 | bytes 34883588 | tf_op jit(solution)/shard_map/while/body/eval_jaxpr/while/body/eval_jaxpr/qhk,shk->hqs/dot_general | solution.py:84
  357.7 10.7 %multiply_convert_fusion.3 = bf16[4,512,2048]{2,1,0:T(8,128)(2,1)} fusion(f32[4,512,2048]{2,1,0:T(8,128)} %get-tuple-element.553, f32[4,512,2048]{2,1,0:T(8,128)S(1)} %fusion.154, f32[4,512]{1,0:T(4,128)S(1)} %get-tuple-element.554, f32[4,512]{1,0:T(4,128)S(1)} %dynamic-slice_bitcast_fusion.2, pred[2048]{0:T(1024)(128)(4,1)S(1)} %convert_compare_fusion.5), kind=kLoop, calls=%fused_computation.24.clone.1 | loop fusion | flops 25165824 | bytes 41961472 | tf_op jit(solution)/shard_map/while/body/eval_jaxpr/while/body/eval_jaxpr/convert_element_type | solution.py:88
  368.3 6.9 fusion.157
  390.0 9.5 %multiply_reduce_fusion.8 = (f32[4,512]{1,0:T(4,128)S(1)}, f32[4,512,2048]{2,1,0:T(8,128)}) fusion(f32[4,512,2048]{2,1,0:T(8,128)S(1)} %fusion.154, f32[4,512]{1,0:T(4,128)S(1)} %dynamic-slice_bitcast_fusion.2, pred[2048]{0:T(1024)(128)(4,1)S(1)} %convert_compare_fusion.5, bf16[2048,4,64]{0,2,1:T(8,128)(2,1)S(1)} %get-tuple-element.611, ...), kind=kOutput, calls=%fused_computation.25.clone.1 | convolution fusion | flops 557840384 | bytes 34883588 | tf_op jit(solution)/shard_map/while/body/eval_jaxpr/while/body/eval_jaxpr/qhk,shk->hqs/dot_general | solution.py:84
  399.5 10.7 %multiply_convert_fusion.3 = bf16[4,512,2048]{2,1,0:T(8,128)(2,1)} fusion(f32[4,512,2048]{2,1,0:T(8,128)} %get-tuple-element.553, f32[4,512,2048]{2,1,0:T(8,128)S(1)} %fusion.154, f32[4,512]{1,0:T(4,128)S(1)} %get-tuple-element.554, f32[4,512]{1,0:T(4,128)S(1)} %dynamic-slice_bitcast_fusion.2, pred[2048]{0:T(1024)(128)(4,1)S(1)} %convert_compare_fusion.5), kind=kLoop, calls=%fused_computation.24.clone.1 | loop fusion | flops 25165824 | bytes 41961472 | tf_op jit(solution)/shard_map/while/body/eval_jaxpr/while/body/eval_jaxpr/convert_element_type | solution.py:88
  410.2 6.9 fusion.157
  431.9 9.5 %multiply_reduce_fusion.8 = (f32[4,512]{1,0:T(4,128)S(1)}, f32[4,512,2048]{2,1,0:T(8,128)}) fusion(f32[4,512,2048]{2,1,0:T(8,128)S(1)} %fusion.154, f32[4,512]{1,0:T(4,128)S(1)} %dynamic-slice_bitcast_fusion.2, pred[2048]{0:T(1024)(128)(4,1)S(1)} %convert_compare_fusion.5, bf16[2048,4,64]{0,2,1:T(8,128)(2,1)S(1)} %get-tuple-element.611, ...), kind=kOutput, calls=%fused_computation.25.clone.1 | convolution fusion | flops 557840384 | bytes 34883588 | tf_op jit(solution)/shard_map/while/body/eval_jaxpr/while/body/eval_jaxpr/qhk,shk->hqs/dot_general | solution.py:84
  441.4 10.7 %multiply_convert_fusion.3 = bf16[4,512,2048]{2,1,0:T(8,128)(2,1)} fusion(f32[4,512,2048]{2,1,0:T(8,128)} %get-tuple-element.553, f32[4,512,2048]{2,1,0:T(8,128)S(1)} %fusion.154, f32[4,512]{1,0:T(4,128)S(1)} %get-tuple-element.554, f32[4,512]{1,0:T(4,128)S(1)} %dynamic-slice_bitcast_fusion.2, pred[2048]{0:T(1024)(128)(4,1)S(1)} %convert_compare_fusion.5), kind=kLoop, calls=%fused_computation.24.clone.1 | loop fusion | flops 25165824 | bytes 41961472 | tf_op jit(solution)/shard_map/while/body/eval_jaxpr/while/body/eval_jaxpr/convert_element_type | solution.py:88
  452.1 6.9 fusion.157
  490.6 17.5 %scatter_custom_fusion = f32[12800,256]{1,0:T(8,128)} fusion(s32[2048]{0:T(1024)S(1)} %bitcast.187, f32[2048,256]{1,0:T(8,128)} %copy.90, f32[]{:T(128)} %constant.51.clone.1), kind=kCustom, calls=%fused_computation.57 | custom fusion | flops 524288 | bytes 13107712 | tf_op jit(solution)/shard_map/scatter-add | solution.py:281
  513.3 26.0 %reduce-scatter.15.cloned.1.call-done = f32[512,256]{0,1:T(8,128)} async-done(((f32[2048,256]{0,1:T(8,128)}), f32[512,256]{0,1:T(8,128)}) %reduce-scatter.15.cloned.1.call-update) | async-done | bytes 524304 | tf_op jit(solution)/shard_map/reduce_scatter | solution.py:307
  539.2 222.0 %reduce-scatter.9.cloned.1.call-done = f32[3200,256]{1,0:T(8,128)} async-done(((f32[12800,256]{1,0:T(8,128)}), f32[3200,256]{1,0:T(8,128)}) %reduce-scatter.9.cloned.1.call-update) | async-done | bytes 3276816 | tf_op jit(solution)/shard_map/reduce_scatter | solution.py:303
  761.3 11.3 %scatter_custom_fusion.1 = f32[12800]{0:T(1024)S(1)} fusion(s32[2048]{0:T(1024)S(1)} %bitcast.188, f32[2048]{0:T(1024)S(1)} %copy-done.36, f32[]{:T(128)} %constant.51.clone.1), kind=kCustom, calls=%fused_computation.126 | custom fusion | flops 2048 | bytes 51204 | tf_op jit(solution)/shard_map/scatter-add | solution.py:282
  780.6 19.4 %all-reduce.20 = (f32[12800]{0:T(1024)S(1)}, f32[256]{0:T(256)S(1)}, f32[256]{0:T(256)S(1)}, f32[256]{0:T(256)S(1)}, f32[256]{0:T(256)S(1)}, /*index=5*/f32[256]...) all-reduce(f32[12800]{0:T(1024)S(1)} %scatter_custom_fusion.1, ...), channel_id=3, replica_groups=mesh['dp'=8,'fsdp'=4] {'fsdp'}, use_global_device_ids=true, to_apply=%region_19.20.clone | all-reduce | flops 15360 | bytes 122880
  804.2 25.4 %all-reduce.18 = (f32[3200]{0:T(1024)S(1)}, f32[16,256]{1,0:T(8,128)}, f32[16,256]{1,0:T(8,128)}, f32[64]{0:T(128)}, f32[64]{0:T(128)}, /*index=5*/f32[64]{0:T(1...) all-reduce(f32[3200]{0:T(1024)S(1)} %dynamic-slice.14, ...), channel_id=1, replica_groups=mesh['dp'=8,'fsdp'=4] {'dp'}, use_global_device_ids=true, to_apply=%region_20.21 | all-reduce | flops 12032 | bytes 96256 | tf_op jit(solution)/shard_map/psum | solution.py:341
  830.2 60.0 %all-reduce.24.cloned.1.call-done = (f32[3200,256]{1,0:T(8,128)}, f32[512,256]{0,1:T(8,128)}, f32[64,768]{1,0:T(8,128)}, f32[64,256]{1,0:T(8,128)}, f32[64,512]{1,0:T(8,128)}, /*index=5*/f32[128,256]{1,0:T(8,128)}) async-done(((f32[3200,256]{1,0:T(8,128)}, f32[512,256]{0,1:T(8,128)}, f32[64,768]{1,0:T(8,128)}, f32[64,256]{1,0:T(8,128)}, f32[64,512]{1,0:T(8,128)}, /*index=5*/f32[128,256]{1,0:T(8,128)}), ...) | async-done | bytes 4325392 | tf_op jit(solution)/shard_map/psum | solution.py:341
  (332 shorter events, 234.4 us)
Async XLA Ops:
  7.2 160.6 %all-gather.4.cloned.1.call-start = ((), (), s32[]{:S(2)}) async-start(), calls=%async_computation.8 | async-start | bytes 8192000 | tf_op jit(solution)/shard_map/all_gather | solution.py:156
  7.9 173.8 %all-gather.6.cloned.1.call-start = ((), (), s32[]{:S(2)}) async-start(), calls=%async_computation.9 | async-start | bytes 1310720 | tf_op jit(solution)/shard_map/all_gather | solution.py:159
  9.8 503.4 %reduce-scatter.19.cloned.1.call-start = ((), (), s32[]{:S(2)}) async-start(), calls=%async_computation.15 | async-start | bytes 327680 | tf_op jit(solution)/shard_map/reduce_scatter | solution.py:313
  65.2 8.2 copy-start.27
  72.7 19.5 %copy-start.49 = (bf16[64,256]{1,0:T(8,128)(2,1)S(1)}, bf16[64,256]{1,0:T(8,128)(2,1)}, u32[]{:S(2)}) copy-start(bf16[64,256]{1,0:T(8,128)(2,1)} %param.42) | copy-start | bytes 98308
  72.7 38.4 %copy-start.44 = (bf16[64,512]{1,0:T(8,128)(2,1)S(1)}, bf16[64,512]{1,0:T(8,128)(2,1)}, u32[]{:S(2)}) copy-start(bf16[64,512]{1,0:T(8,128)(2,1)} %param.46) | copy-start | bytes 196612
  72.7 60.5 %copy-start.45 = (bf16[128,256]{1,0:T(8,128)(2,1)S(1)}, bf16[128,256]{1,0:T(8,128)(2,1)}, u32[]{:S(2)}) copy-start(bf16[128,256]{1,0:T(8,128)(2,1)} %param.48) | copy-start | bytes 196612
  73.4 94.4 %copy-start.50 = (s32[1,2048]{1,0:T(1,128)S(1)}, s32[1,2048]{1,0:T(1,128)}, u32[]{:S(2)}) copy-start(s32[1,2048]{1,0:T(1,128)} %param.27) | copy-start | bytes 24580
  150.7 31.0 %copy-start.34 = (f32[2048]{0:T(1024)}, f32[2048]{0:T(1024)S(1)}, u32[]{:S(2)}) copy-start(f32[2048]{0:T(1024)S(1)} %fusion.78) | copy-start | bytes 24580
  167.8 16.4 %copy-start.20 = (bf16[256,768]{1,0:T(8,128)(2,1)}, bf16[256,768]{1,0:T(8,128)(2,1)S(1)}, u32[]{:S(2)}) copy-start(bf16[256,768]{1,0:T(8,128)(2,1)S(1)} %all_gather.63) | copy-start | bytes 1179652
  167.8 13.9 %copy-start.63 = (f32[1,256]{1,0:T(1,128)S(1)}, f32[1,256]{1,0:T(1,128)}, u32[]{:S(2)}) copy-start(f32[1,256]{1,0:T(1,128)} %dynamic-slice_convert_fusion) | copy-start | bytes 3076
  248.9 11.5 %copy-start.4 = (f32[2048,256]{0,1:T(8,128)}, f32[2048,256]{0,1:T(8,128)S(1)}, u32[]{:S(2)}) copy-start(f32[2048,256]{0,1:T(8,128)S(1)} %get-tuple-element.435) | copy-start | bytes 6291460
  249.5 11.0 %copy-start.15 = (bf16[1,2048,256]{1,2,0:T(8,128)(2,1)S(1)}, bf16[1,2048,256]{1,2,0:T(8,128)(2,1)}, u32[]{:S(2)}) copy-start(bf16[1,2048,256]{1,2,0:T(8,128)(2,1)} %copy.83) | copy-start | bytes 3145732
  249.5 11.0 %copy-start.24 = (bf16[512,256]{1,0:T(8,128)(2,1)S(1)}, bf16[512,256]{1,0:T(8,128)(2,1)}, u32[]{:S(2)}) copy-start(bf16[512,256]{1,0:T(8,128)(2,1)} %all_gather.72) | copy-start | bytes 786436
  249.5 11.0 %copy-start.35 = (f32[2048]{0:T(1024)S(1)}, f32[2048]{0:T(1024)}, u32[]{:S(2)}) copy-start(f32[2048]{0:T(1024)} %copy-done.34) | copy-start | bytes 24580
  278.0 235.2 %reduce-scatter.21.cloned.1.call-start = ((), (), s32[]{:S(2)}) async-start(), calls=%async_computation.16 | async-start | bytes 655360 | tf_op jit(solution)/shard_map/reduce_scatter | solution.py:317
  281.9 231.4 %reduce-scatter.23.cloned.1.call-start = ((), (), s32[]{:S(2)}) async-start(), calls=%async_computation.17 | async-start | bytes 655360 | tf_op jit(solution)/shard_map/reduce_scatter | solution.py:319
  296.9 216.3 %reduce-scatter.17.cloned.1.call-start = ((), (), s32[]{:S(2)}) async-start(), calls=%async_computation.14 | async-start | bytes 983040 | tf_op jit(solution)/shard_map/reduce_scatter | solution.py:310
  327.1 6.9 copy-start
  368.3 6.9 copy-start
  410.2 6.9 copy-start
  452.1 6.9 copy-start
  472.8 66.5 %reduce-scatter.15.cloned.1.call-start = ((), (), s32[]{:S(2)}) async-start(), calls=%async_computation.13 | async-start | bytes 2621440 | tf_op jit(solution)/shard_map/reduce_scatter | solution.py:307
  487.2 274.0 %reduce-scatter.9.cloned.1.call-start = ((), (), s32[]{:S(2)}) async-start(), calls=%async_computation.10 | async-start | bytes 16384000 | tf_op jit(solution)/shard_map/reduce_scatter | solution.py:303
  508.1 292.7 %reduce-scatter.13.cloned.1.call-start = ((), (), s32[]{:S(2)}) async-start(), calls=%async_computation.12 | async-start | bytes 81920 | tf_op jit(solution)/shard_map/reduce_scatter | solution.py:306
  508.9 295.2 %reduce-scatter.11.cloned.1.call-start = ((), (), s32[]{:S(2)}) async-start(), calls=%async_computation.11 | async-start | bytes 81920 | tf_op jit(solution)/shard_map/reduce_scatter | solution.py:305
  509.2 265.3 %copy-start.71 = (bf16[256]{0:T(256)(128)(2,1)S(1)}, bf16[256]{0:T(256)(128)(2,1)}, u32[]{:S(2)}) copy-start(bf16[256]{0:T(256)(128)(2,1)} %get-tuple-element.412) | copy-start | bytes 1540
  509.2 265.3 %copy-start.6 = (f32[2048,256]{0,1:T(8,128)S(1)}, f32[2048,256]{0,1:T(8,128)}, u32[]{:S(2)}) copy-start(f32[2048,256]{0,1:T(8,128)} %copy-done.4) | copy-start | bytes 6291460
  509.2 265.3 %copy-start.25 = (bf16[512,256]{1,0:T(8,128)(2,1)S(1)}, bf16[512,256]{1,0:T(8,128)(2,1)}, u32[]{:S(2)}) copy-start(bf16[512,256]{1,0:T(8,128)(2,1)} %all_gather.72) | copy-start | bytes 786436
  513.1 377.1 %all-reduce.24.cloned.1.call-start = ((), (), s32[]{:S(2)}) async-start(), calls=%async_computation.18 | async-start | bytes 8650752 | tf_op jit(solution)/shard_map/psum | solution.py:341
  774.5 6.1 copy-start.57
  774.5 6.1 copy-start.60
  (55 other events, 160.1 us)
Sparse Core Ops, SparseCore 0:
  9.6 133.5 all-gather.3
  145.3 29.6 all-gather.5
  278.1 16.6 reduce-scatter.18
  297.6 19.8 reduce-scatter.20
  319.8 19.8 reduce-scatter.22
  472.9 20.1 reduce-scatter.16
  496.1 43.1 reduce-scatter.14
  541.6 219.6 reduce-scatter.8
  764.1 20.0 reduce-scatter.12
  786.9 17.1 reduce-scatter.10
  808.0 82.1 all-reduce.23
where the time goes:
time: 911 us; the launch traced here: 906 us
  waiting for transfers between devices  312 us (34%)
  matrix products  201 us (22%)
  blocking collectives  176 us (19%)
  other arithmetic  119 us (13%)
  local copies, waits for them, and re-layouts  77.5 us (9%)
  between operations  19.1 us (2%)
    reduce_scatter x1, waiting for transfers between devices, body(): lax.psum_scatter(dense_grad, 'fsdp', scatter_dimension=0, tiled=True)  222 us
    psum x1, waiting for transfers between devices, body(): lax.psum((table_share, count_share, expr_share, study_share, position_sha...  60 us
    convert_element_type x4, other arithmetic, one_block(): grad_scores = (probs * (grad_probs - inner)).astype(jnp.bfloat16)  42.7 us
    dot_general x4, matrix products, one_block(): jnp.einsum('qhk,shk->hqs', grad_block, values, preferred_element_type=jnp...  38.1 us
    unnamed x185, local copies, waits for them, and re-layouts  37.2 us
    unnamed x2, blocking collectives  35.6 us
    dot_general x4, matrix products, one_block(): jnp.einsum('hqs,shk->qhk', grad_scores, keys, preferred_element_type=jnp....  27.6 us
    dot_general x8, matrix products, one_block(): jnp.einsum('qhk,shk->hqs', query_block, keys, preferred_element_type=jnp....  27.3 us
  transfers between devices with their start and end apart: 11, of which 4 were waited for; matrix products, arithmetic and copies ran while one was open for 32% of the time, Pallas kernels for 0%

commit v1 on v0

--- a/solution.py
+++ b/solution.py
@@ -6,6 +6,27 @@
 HEADS = 4
 epsilon = 1e-05
 highest = lax.Precision.HIGHEST
+
+
+def joined_along(blocks, dim):
+    dims = list(blocks.shape[1:])
+    dims[dim] *= blocks.shape[0]
+    return jnp.moveaxis(blocks, 0, dim).reshape(dims)
+
+
+def collected_by_bits(array, axis):
+    size, mine = (lax.axis_size(axis), lax.axis_index(axis))
+    blocks, stride = (array[None], 1)
+    while stride < size:
+        theirs = lax.ppermute(blocks, axis, [(i, i ^ stride) for i in range(size)])
+        low = mine & stride == 0
+        blocks = jnp.concatenate([jnp.where(low, blocks, theirs), jnp.where(low, theirs, blocks)])
+        stride *= 2
+    return blocks
+
+
+def collect(x, axis, dim):
+    return joined_along(collected_by_bits(x, axis), dim)
 
 
 def normalize(values):
@@ -162,7 +183,7 @@
         lax.all_gather(w_qkv, "fsdp", axis=0, tiled=True),
         lax.all_gather(bias_query, "fsdp", axis=0, tiled=True),
         lax.all_gather(bias_value, "fsdp", axis=0, tiled=True),
-        lax.all_gather(w_output, "fsdp", axis=0, tiled=True),
+        collect(w_output, "fsdp", 0),
         lax.all_gather(bias_output, "fsdp", axis=0, tiled=True),
         lax.all_gather(norm2_gain, "fsdp", axis=0, tiled=True),
         lax.all_gather(norm2_shift, "fsdp", axis=0, tiled=True),

time: 911 us -> 925 us (1.015)
  waiting for transfers between devices: 312 us -> 327 us
    all_gather x1, waiting for transfers between devices: 0.02 us -> 12.7 us  [body(): lax.all_gather(position_table, 'fsdp', axis=0, tiled=True)]
    unnamed x185 -> x197, local copies, waits for them, and re-layouts: 37.2 us -> 31.5 us
  transfers between devices with their start and end apart: 11 -> 13, of which waited for: 4 -> 5; matrix products, arithmetic and copies ran while one was open for 32% -> 31% of each run, Pallas kernels for 0% -> 0%
where the time goes in v1:
time: 925 us; the launch traced here: 919 us
  waiting for transfers between devices  327 us (35%)
  matrix products  201 us (22%)
  blocking collectives  172 us (19%)
  other arithmetic  122 us (13%)
  local copies, waits for them, and re-layouts  71.9 us (8%)
  between operations  19.1 us (2%)
    reduce_scatter x1, waiting for transfers between devices, body(): lax.psum_scatter(dense_grad, 'fsdp', scatter_dimension=0, tiled=True)  222 us
    psum x1, waiting for transfers between devices, body(): lax.psum((table_share, count_share, expr_share, study_share, position_sha...  60.2 us
    convert_element_type x4, other arithmetic, one_block(): grad_scores = (probs * (grad_probs - inner)).astype(jnp.bfloat16)  42.9 us
    dot_general x4, matrix products, one_block(): jnp.einsum('qhk,shk->hqs', grad_block, values, preferred_element_type=jnp...  38 us
    unnamed x197, local copies, waits for them, and re-layouts  31.5 us
    unnamed x2, blocking collectives  29.2 us
    reduce_scatter x1, waiting for transfers between devices, body(): lax.psum_scatter(grad_position, 'fsdp', scatter_dimension=0, tiled=True)  28.3 us
    dot_general x4, matrix products, one_block(): jnp.einsum('hqs,shk->qhk', grad_scores, keys, preferred_element_type=jnp....  27.6 us
  transfers between devices with their start and end apart: 13, of which 5 were waited for; matrix products, arithmetic and copies ran while one was open for 31% of the time, Pallas kernels for 0%

profile of v1, /device:TPU:0, one launch (start us, length us, event | category | flops | bytes accessed | tf_op | source)
XLA Modules:
  0.0 918.7 jit_solution(10447657815320737999)
XLA Ops:
  15.1 13.7 %all_gather.58 = bf16[64,256]{1,0:T(8,128)(2,1)S(1)} all-gather(bf16[16,256]{1,0:T(8,128)(2,1)} %param.35), channel_id=1, replica_groups=mesh['dp'=8,'fsdp'=4] {'fsdp'}, dimensions={0}, use_global_device_ids=true | all-gather | bytes 40960 | tf_op jit(solution)/shard_map/all_gather | solution.py:179
  28.8 21.9 %all_gather.62 = bf16[256,768]{1,0:T(8,128)(2,1)S(1)} all-gather(bf16[64,768]{1,0:T(8,128)(2,1)} %param.39), channel_id=1, replica_groups=mesh['dp'=8,'fsdp'=4] {'fsdp'}, dimensions={0}, use_global_device_ids=true | all-gather | bytes 491520 | tf_op jit(solution)/shard_map/all_gather | solution.py:183
  52.0 20.5 %all_gather.68 = bf16[256,512]{1,0:T(8,128)(2,1)} all-gather(bf16[64,512]{1,0:T(8,128)(2,1)} %param.46), channel_id=1, replica_groups=mesh['dp'=8,'fsdp'=4] {'fsdp'}, dimensions={0}, use_global_device_ids=true | all-gather | bytes 327680 | tf_op jit(solution)/shard_map/all_gather | solution.py:190
  75.7 9.8 %all-reduce.21 = (bf16[256]{0:T(256)(128)(2,1)S(1)}, bf16[256]{0:T(256)(128)(2,1)S(1)}, bf16[256]{0:T(256)(128)(2,1)S(1)}, bf16[256]{0:T(256)(128)(2,1)S(1)}, bf...) all-reduce(bf16[256]{0:T(256)(128)(2,1)S(1)} %dynamic-update-slice., ...), channel_id=1, replica_groups=mesh['dp'=8,'fsdp'=4] {'fsdp'}, use_global_device_ids=true, to_apply=%add.1 | all-reduce | flops 2048 | bytes 8192
  89.4 12.9 %all-gather = bf16[4,1,128]{2,1,0:T(2,128)(2,1)S(1)} all-gather(bf16[1,1,128]{2,1,0:T(2,128)(2,1)S(1)} %bitcast.198), channel_id=1, replica_groups=mesh['dp'=8,'fsdp'=4] {'fsdp'}, dimensions={0}, use_global_device_ids=true | all-gather | bytes 1280 | tf_op jit(solution)/shard_map/all_gather | solution.py:191
  102.9 16.0 %all_gather.57 = bf16[64,256]{1,0:T(8,128)(2,1)S(1)} all-gather(bf16[16,256]{1,0:T(8,128)(2,1)S(1)} %copy-done.52), channel_id=1, replica_groups=mesh['dp'=8,'fsdp'=4] {'fsdp'}, dimensions={0}, use_global_device_ids=true | all-gather | bytes 40960 | tf_op jit(solution)/shard_map/all_gather | solution.py:178
  118.9 7.5 gather_fusion.1
  132.7 18.5 %all_gather.70 = bf16[512,256]{1,0:T(8,128)(2,1)} all-gather(bf16[128,256]{1,0:T(8,128)(2,1)} %param.48), channel_id=1, replica_groups=mesh['dp'=8,'fsdp'=4] {'fsdp'}, dimensions={0}, use_global_device_ids=true | all-gather | bytes 327680 | tf_op jit(solution)/shard_map/all_gather | solution.py:192
  151.9 12.2 %gather_fusion = bf16[2048,256]{1,0:T(8,128)(2,1)} fusion(bf16[12800,256]{1,0:T(8,128)(2,1)} %all-gather.4.cloned.1.call-done, s32[2048]{0:T(1024)S(1)} %broadcast_clamp_fusion.1), kind=kCustom, calls=%fused_computation | custom fusion | bytes 2105344 | tf_op jit(solution)/shard_map/gather | solution.py:210
  165.6 12.7 %all-gather.6.cloned.1.call-done = bf16[2048,256]{0,1:T(8,128)(2,1)} async-done(((bf16[512,256]{0,1:T(8,128)(2,1)}), bf16[2048,256]{0,1:T(8,128)(2,1)}) %all-gather.6.cloned.1.call-update) | async-done | bytes 1048592 | tf_op jit(solution)/shard_map/all_gather | solution.py:180
  188.5 53.9 %while.49 = (s32[]{:T(128)}, bf16[4,512,4,64]{1,3,2,0:T(8,128)(2,1)}, f32[4,4,512]{2,1,0:T(4,128)S(1)}, bf16[4,512,4,64]{1,3,2,0:T(8,128)(2,1)}, bf16[2048,4,64]...) while((s32[]{:T(128)}, bf16[4,512,4,64]{1,3,2,0:T(8,128)(2,1)}, ...), condition=%wide.region_5.6_spmd.clone, body=%wide.region_2.5_spmd.clone.sunk | while | flops 1124208640 | bytes 53026924 | solution.py:85
  246.1 10.9 %multiply_convert_fusion.1 = (bf16[2048,512]{1,0:T(8,128)(2,1)}, f32[2048,512]{1,0:T(8,128)S(1)}, f32[2048,512]{1,0:T(8,128)S(1)}) fusion(f32[512]{0:T(512)S(1)} %bitcast.196, bf16[256,512]{1,0:T(8,128)(2,1)S(1)} %copy-done.25, f32[2048,256]{0,1:T(8,128)S(1)} %get-tuple-element.439, f32[256]{0:T(256)S(1)} %copy-done.78, f32[256]{0:T(256)S(1)} %copy-done.60, ...), kind=kOutput, calls=%fused_computation.63 | convolution fusion | flops 608698368 | bytes 12865536 | tf_op jit(solution)/shard_map/dot_general | solution.py:46
  278.6 14.0 %all_gather.72 = bf16[256,256]{1,0:T(8,128)(2,1)S(1)} all-gather(bf16[64,256]{1,0:T(8,128)(2,1)S(1)} %copy-done.40), channel_id=1, replica_groups=mesh['dp'=8,'fsdp'=4] {'fsdp'}, dimensions={0}, use_global_device_ids=true | all-gather | bytes 163840 | tf_op jit(solution)/shard_map/all_gather | solution.py:243
  307.6 166.9 %while.50 = (s32[]{:T(128)}, f32[2048,4,64]{0,2,1:T(8,128)}, f32[2048,4,64]{0,2,1:T(8,128)}, bf16[4,512,4,64]{1,3,2,0:T(8,128)(2,1)}, bf16[4,512,4,64]{1,3,2,0:T...) while((s32[]{:T(128)}, f32[2048,4,64]{0,2,1:T(8,128)}, ...), condition=%wide.region_12.13_spmd.clone, body=%wide.region_10.12_spmd.clone.sunk | while | flops 2750025728 | bytes 172556464 | solution.py:127
  317.4 9.5 %multiply_reduce_fusion.8 = (f32[4,512]{1,0:T(4,128)S(1)}, f32[4,512,2048]{2,1,0:T(8,128)}) fusion(f32[4,512,2048]{2,1,0:T(8,128)S(1)} %fusion.154, f32[4,512]{1,0:T(4,128)S(1)} %dynamic-slice_bitcast_fusion.2, pred[2048]{0:T(1024)(128)(4,1)S(1)} %convert_compare_fusion.5, bf16[2048,4,64]{0,2,1:T(8,128)(2,1)S(1)} %get-tuple-element.615, ...), kind=kOutput, calls=%fused_computation.25.clone.1 | convolution fusion | flops 557840384 | bytes 34883588 | tf_op jit(solution)/shard_map/while/body/eval_jaxpr/while/body/eval_jaxpr/qhk,shk->hqs/dot_general | solution.py:105
  326.9 10.7 %multiply_convert_fusion.3 = bf16[4,512,2048]{2,1,0:T(8,128)(2,1)} fusion(f32[4,512,2048]{2,1,0:T(8,128)} %get-tuple-element.557, f32[4,512,2048]{2,1,0:T(8,128)S(1)} %fusion.154, f32[4,512]{1,0:T(4,128)S(1)} %get-tuple-element.558, f32[4,512]{1,0:T(4,128)S(1)} %dynamic-slice_bitcast_fusion.2, pred[2048]{0:T(1024)(128)(4,1)S(1)} %convert_compare_fusion.5), kind=kLoop, calls=%fused_computation.24.clone.1 | loop fusion | flops 25165824 | bytes 41961472 | tf_op jit(solution)/shard_map/while/body/eval_jaxpr/while/body/eval_jaxpr/convert_element_type | solution.py:109
  337.7 6.9 fusion.157
  358.7 9.5 %multiply_reduce_fusion.8 = (f32[4,512]{1,0:T(4,128)S(1)}, f32[4,512,2048]{2,1,0:T(8,128)}) fusion(f32[4,512,2048]{2,1,0:T(8,128)S(1)} %fusion.154, f32[4,512]{1,0:T(4,128)S(1)} %dynamic-slice_bitcast_fusion.2, pred[2048]{0:T(1024)(128)(4,1)S(1)} %convert_compare_fusion.5, bf16[2048,4,64]{0,2,1:T(8,128)(2,1)S(1)} %get-tuple-element.615, ...), kind=kOutput, calls=%fused_computation.25.clone.1 | convolution fusion | flops 557840384 | bytes 34883588 | tf_op jit(solution)/shard_map/while/body/eval_jaxpr/while/body/eval_jaxpr/qhk,shk->hqs/dot_general | solution.py:105
  368.2 10.7 %multiply_convert_fusion.3 = bf16[4,512,2048]{2,1,0:T(8,128)(2,1)} fusion(f32[4,512,2048]{2,1,0:T(8,128)} %get-tuple-element.557, f32[4,512,2048]{2,1,0:T(8,128)S(1)} %fusion.154, f32[4,512]{1,0:T(4,128)S(1)} %get-tuple-element.558, f32[4,512]{1,0:T(4,128)S(1)} %dynamic-slice_bitcast_fusion.2, pred[2048]{0:T(1024)(128)(4,1)S(1)} %convert_compare_fusion.5), kind=kLoop, calls=%fused_computation.24.clone.1 | loop fusion | flops 25165824 | bytes 41961472 | tf_op jit(solution)/shard_map/while/body/eval_jaxpr/while/body/eval_jaxpr/convert_element_type | solution.py:109
  378.9 6.9 fusion.157
  400.6 9.5 %multiply_reduce_fusion.8 = (f32[4,512]{1,0:T(4,128)S(1)}, f32[4,512,2048]{2,1,0:T(8,128)}) fusion(f32[4,512,2048]{2,1,0:T(8,128)S(1)} %fusion.154, f32[4,512]{1,0:T(4,128)S(1)} %dynamic-slice_bitcast_fusion.2, pred[2048]{0:T(1024)(128)(4,1)S(1)} %convert_compare_fusion.5, bf16[2048,4,64]{0,2,1:T(8,128)(2,1)S(1)} %get-tuple-element.615, ...), kind=kOutput, calls=%fused_computation.25.clone.1 | convolution fusion | flops 557840384 | bytes 34883588 | tf_op jit(solution)/shard_map/while/body/eval_jaxpr/while/body/eval_jaxpr/qhk,shk->hqs/dot_general | solution.py:105
  410.1 10.7 %multiply_convert_fusion.3 = bf16[4,512,2048]{2,1,0:T(8,128)(2,1)} fusion(f32[4,512,2048]{2,1,0:T(8,128)} %get-tuple-element.557, f32[4,512,2048]{2,1,0:T(8,128)S(1)} %fusion.154, f32[4,512]{1,0:T(4,128)S(1)} %get-tuple-element.558, f32[4,512]{1,0:T(4,128)S(1)} %dynamic-slice_bitcast_fusion.2, pred[2048]{0:T(1024)(128)(4,1)S(1)} %convert_compare_fusion.5), kind=kLoop, calls=%fused_computation.24.clone.1 | loop fusion | flops 25165824 | bytes 41961472 | tf_op jit(solution)/shard_map/while/body/eval_jaxpr/while/body/eval_jaxpr/convert_element_type | solution.py:109
  420.9 6.9 fusion.157
  442.6 9.5 %multiply_reduce_fusion.8 = (f32[4,512]{1,0:T(4,128)S(1)}, f32[4,512,2048]{2,1,0:T(8,128)}) fusion(f32[4,512,2048]{2,1,0:T(8,128)S(1)} %fusion.154, f32[4,512]{1,0:T(4,128)S(1)} %dynamic-slice_bitcast_fusion.2, pred[2048]{0:T(1024)(128)(4,1)S(1)} %convert_compare_fusion.5, bf16[2048,4,64]{0,2,1:T(8,128)(2,1)S(1)} %get-tuple-element.615, ...), kind=kOutput, calls=%fused_computation.25.clone.1 | convolution fusion | flops 557840384 | bytes 34883588 | tf_op jit(solution)/shard_map/while/body/eval_jaxpr/while/body/eval_jaxpr/qhk,shk->hqs/dot_general | solution.py:105
  452.1 10.7 %multiply_convert_fusion.3 = bf16[4,512,2048]{2,1,0:T(8,128)(2,1)} fusion(f32[4,512,2048]{2,1,0:T(8,128)} %get-tuple-element.557, f32[4,512,2048]{2,1,0:T(8,128)S(1)} %fusion.154, f32[4,512]{1,0:T(4,128)S(1)} %get-tuple-element.558, f32[4,512]{1,0:T(4,128)S(1)} %dynamic-slice_bitcast_fusion.2, pred[2048]{0:T(1024)(128)(4,1)S(1)} %convert_compare_fusion.5), kind=kLoop, calls=%fused_computation.24.clone.1 | loop fusion | flops 25165824 | bytes 41961472 | tf_op jit(solution)/shard_map/while/body/eval_jaxpr/while/body/eval_jaxpr/convert_element_type | solution.py:109
  501.4 17.5 %scatter_custom_fusion = f32[12800,256]{1,0:T(8,128)} fusion(s32[2048]{0:T(1024)S(1)} %bitcast.193, f32[2048,256]{1,0:T(8,128)} %copy.90, f32[]{:T(128)} %constant.50.clone.1), kind=kCustom, calls=%fused_computation.57 | custom fusion | flops 524288 | bytes 13107712 | tf_op jit(solution)/shard_map/scatter-add | solution.py:302
  524.1 28.3 %reduce-scatter.15.cloned.1.call-done = f32[512,256]{0,1:T(8,128)} async-done(((f32[2048,256]{0,1:T(8,128)}), f32[512,256]{0,1:T(8,128)}) %reduce-scatter.15.cloned.1.call-update) | async-done | bytes 524304 | tf_op jit(solution)/shard_map/reduce_scatter | solution.py:328
  552.3 222.0 %reduce-scatter.9.cloned.1.call-done = f32[3200,256]{1,0:T(8,128)} async-done(((f32[12800,256]{1,0:T(8,128)}), f32[3200,256]{1,0:T(8,128)}) %reduce-scatter.9.cloned.1.call-update) | async-done | bytes 3276816 | tf_op jit(solution)/shard_map/reduce_scatter | solution.py:324
  774.4 11.3 %scatter_custom_fusion.1 = f32[12800]{0:T(1024)S(1)} fusion(s32[2048]{0:T(1024)S(1)} %bitcast.194, f32[2048]{0:T(1024)S(1)} %copy-done.36, f32[]{:T(128)} %constant.50.clone.1), kind=kCustom, calls=%fused_computation.132 | custom fusion | flops 2048 | bytes 51204 | tf_op jit(solution)/shard_map/scatter-add | solution.py:303
  793.7 19.4 %all-reduce.20 = (f32[12800]{0:T(1024)S(1)}, f32[256]{0:T(256)S(1)}, f32[256]{0:T(256)S(1)}, f32[256]{0:T(256)S(1)}, f32[256]{0:T(256)S(1)}, /*index=5*/f32[256]...) all-reduce(f32[12800]{0:T(1024)S(1)} %scatter_custom_fusion.1, ...), channel_id=3, replica_groups=mesh['dp'=8,'fsdp'=4] {'fsdp'}, use_global_device_ids=true, to_apply=%region_19.20.clone | all-reduce | flops 15360 | bytes 122880
  817.2 25.4 %all-reduce.18 = (f32[3200]{0:T(1024)S(1)}, f32[16,256]{1,0:T(8,128)}, f32[16,256]{1,0:T(8,128)}, f32[64]{0:T(128)}, f32[64]{0:T(128)}, /*index=5*/f32[64]{0:T(1...) all-reduce(f32[3200]{0:T(1024)S(1)} %dynamic-slice.14, ...), channel_id=1, replica_groups=mesh['dp'=8,'fsdp'=4] {'dp'}, use_global_device_ids=true, to_apply=%region_20.21 | all-reduce | flops 12032 | bytes 96256 | tf_op jit(solution)/shard_map/psum | solution.py:362
  843.2 60.2 %all-reduce.24.cloned.1.call-done = (f32[3200,256]{1,0:T(8,128)}, f32[512,256]{0,1:T(8,128)}, f32[64,768]{1,0:T(8,128)}, f32[64,256]{1,0:T(8,128)}, f32[64,512]{1,0:T(8,128)}, /*index=5*/f32[128,256]{1,0:T(8,128)}) async-done(((f32[3200,256]{1,0:T(8,128)}, f32[512,256]{0,1:T(8,128)}, f32[64,768]{1,0:T(8,128)}, f32[64,256]{1,0:T(8,128)}, f32[64,512]{1,0:T(8,128)}, /*index=5*/f32[128,256]{1,0:T(8,128)}), ...) | async-done | bytes 4325392 | tf_op jit(solution)/shard_map/psum | solution.py:362
  (352 shorter events, 243.0 us)
Async XLA Ops:
  7.2 65.3 %copy-start.62 = (u32[32]{0:T(128)S(1)}, u32[32]{0:T(128)}, u32[]{:S(2)}) copy-start(u32[32]{0:T(128)} %constant.209) | copy-start | bytes 388
  7.2 66.5 %copy-start.69 = (bf16[64]{0:T(256)(128)(2,1)S(1)}, bf16[64]{0:T(256)(128)(2,1)}, u32[]{:S(2)}) copy-start(bf16[64]{0:T(256)(128)(2,1)} %param.44) | copy-start | bytes 388
  7.2 66.8 %copy-start.70 = (bf16[64]{0:T(256)(128)(2,1)S(1)}, bf16[64]{0:T(256)(128)(2,1)}, u32[]{:S(2)}) copy-start(bf16[64]{0:T(256)(128)(2,1)} %param.45) | copy-start | bytes 388
  7.2 67.0 %copy-start.71 = (bf16[64]{0:T(256)(128)(2,1)S(1)}, bf16[64]{0:T(256)(128)(2,1)}, u32[]{:S(2)}) copy-start(bf16[64]{0:T(256)(128)(2,1)} %param.43) | copy-start | bytes 388
  7.2 67.3 %copy-start.72 = (bf16[64]{0:T(256)(128)(2,1)S(1)}, bf16[64]{0:T(256)(128)(2,1)}, u32[]{:S(2)}) copy-start(bf16[64]{0:T(256)(128)(2,1)} %param.41) | copy-start | bytes 388
  7.2 67.5 %copy-start.73 = (bf16[64]{0:T(256)(128)(2,1)S(1)}, bf16[64]{0:T(256)(128)(2,1)}, u32[]{:S(2)}) copy-start(bf16[64]{0:T(256)(128)(2,1)} %param.40) | copy-start | bytes 388
  7.3 67.7 %copy-start.74 = (bf16[64]{0:T(256)(128)(2,1)S(1)}, bf16[64]{0:T(256)(128)(2,1)}, u32[]{:S(2)}) copy-start(bf16[64]{0:T(256)(128)(2,1)} %param.37) | copy-start | bytes 388
  7.3 68.0 %copy-start.75 = (bf16[64]{0:T(256)(128)(2,1)S(1)}, bf16[64]{0:T(256)(128)(2,1)}, u32[]{:S(2)}) copy-start(bf16[64]{0:T(256)(128)(2,1)} %param.38) | copy-start | bytes 388
  7.3 68.2 %copy-start.76 = (bf16[64]{0:T(256)(128)(2,1)S(1)}, bf16[64]{0:T(256)(128)(2,1)}, u32[]{:S(2)}) copy-start(bf16[64]{0:T(256)(128)(2,1)} %param.49) | copy-start | bytes 388
  7.3 82.1 %copy-start.68 = (bf16[128]{0:T(256)(128)(2,1)S(1)}, bf16[128]{0:T(256)(128)(2,1)}, u32[]{:S(2)}) copy-start(bf16[128]{0:T(256)(128)(2,1)} %param.47) | copy-start | bytes 772
  7.3 95.6 %copy-start.52 = (bf16[16,256]{1,0:T(8,128)(2,1)S(1)}, bf16[16,256]{1,0:T(8,128)(2,1)}, u32[]{:S(2)}) copy-start(bf16[16,256]{1,0:T(8,128)(2,1)} %param.34) | copy-start | bytes 24580
  7.3 144.6 %all-gather.4.cloned.1.call-start = ((), (), s32[]{:S(2)}) async-start(), calls=%async_computation.8 | async-start | bytes 8192000 | tf_op jit(solution)/shard_map/all_gather | solution.py:177
  8.0 170.3 %all-gather.6.cloned.1.call-start = ((), (), s32[]{:S(2)}) async-start(), calls=%async_computation.9 | async-start | bytes 1310720 | tf_op jit(solution)/shard_map/all_gather | solution.py:180
  8.1 121.9 %collective-permute-start = (bf16[1,64,256]{2,1,0:T(8,128)(2,1)}, bf16[1,64,256]{2,1,0:T(8,128)(2,1)}, u32[]{:S(2)}, u32[]{:S(2)}) collective-permute-start(bf16[1,64,256]{2,1,0:T(8,128)(2,1)} %bitcast.189), channel_id=1, source_target_pairs={{0,1},{1,0},{2,3},{3,2},{4,5},{5,4},{6,7},{7,6},{8,9},{9,8},{10,11... | collective-permute-start | bytes 98312 | tf_op jit(solution)/shard_map/ppermute | solution.py:21
  13.0 511.0 %reduce-scatter.19.cloned.1.call-start = ((), (), s32[]{:S(2)}) async-start(), calls=%async_computation.15 | async-start | bytes 327680 | tf_op jit(solution)/shard_map/reduce_scatter | solution.py:334
  14.4 164.0 %copy-start.34 = (f32[2048]{0:T(1024)}, f32[2048]{0:T(1024)S(1)}, u32[]{:S(2)}) copy-start(f32[2048]{0:T(1024)S(1)} %fusion.78) | copy-start | bytes 24580
  50.7 130.1 %copy-start.20 = (bf16[256,768]{1,0:T(8,128)(2,1)}, bf16[256,768]{1,0:T(8,128)(2,1)S(1)}, u32[]{:S(2)}) copy-start(bf16[256,768]{1,0:T(8,128)(2,1)S(1)} %all_gather.62) | copy-start | bytes 1179652
  130.8 20.4 %collective-permute-start.1 = (bf16[2,64,256]{2,1,0:T(8,128)(2,1)S(1)}, bf16[2,64,256]{2,1,0:T(8,128)(2,1)S(1)}, u32[]{:S(2)}, u32[]{:S(2)}) collective-permute-start(bf16[2,64,256]{2,1,0:T(8,128)(2,1)S(1)} %pad_maximum_fusion.4), channel_id=1, source_target_pairs={{0,2},{1,3},{2,0},{3,1},{4,6},{5,7},{6,4},{7,5},{8,10},{9,11},{10,... | collective-permute-start | bytes 196616 | tf_op jit(solution)/shard_map/ppermute | solution.py:21
  245.5 11.5 %copy-start.4 = (f32[2048,256]{0,1:T(8,128)}, f32[2048,256]{0,1:T(8,128)S(1)}, u32[]{:S(2)}) copy-start(f32[2048,256]{0,1:T(8,128)S(1)} %get-tuple-element.439) | copy-start | bytes 6291460
  246.0 10.9 %copy-start.15 = (bf16[1,2048,256]{1,2,0:T(8,128)(2,1)S(1)}, bf16[1,2048,256]{1,2,0:T(8,128)(2,1)}, u32[]{:S(2)}) copy-start(bf16[1,2048,256]{1,2,0:T(8,128)(2,1)} %copy.83) | copy-start | bytes 3145732
  246.0 10.9 %copy-start.23 = (bf16[512,256]{1,0:T(8,128)(2,1)S(1)}, bf16[512,256]{1,0:T(8,128)(2,1)}, u32[]{:S(2)}) copy-start(bf16[512,256]{1,0:T(8,128)(2,1)} %all_gather.70) | copy-start | bytes 786436
  274.6 249.4 %reduce-scatter.21.cloned.1.call-start = ((), (), s32[]{:S(2)}) async-start(), calls=%async_computation.16 | async-start | bytes 655360 | tf_op jit(solution)/shard_map/reduce_scatter | solution.py:338
  278.5 245.5 %reduce-scatter.23.cloned.1.call-start = ((), (), s32[]{:S(2)}) async-start(), calls=%async_computation.17 | async-start | bytes 655360 | tf_op jit(solution)/shard_map/reduce_scatter | solution.py:340
  307.5 216.5 %reduce-scatter.17.cloned.1.call-start = ((), (), s32[]{:S(2)}) async-start(), calls=%async_computation.14 | async-start | bytes 983040 | tf_op jit(solution)/shard_map/reduce_scatter | solution.py:331
  483.5 68.8 %reduce-scatter.15.cloned.1.call-start = ((), (), s32[]{:S(2)}) async-start(), calls=%async_computation.13 | async-start | bytes 2621440 | tf_op jit(solution)/shard_map/reduce_scatter | solution.py:328
  498.0 276.4 %reduce-scatter.9.cloned.1.call-start = ((), (), s32[]{:S(2)}) async-start(), calls=%async_computation.10 | async-start | bytes 16384000 | tf_op jit(solution)/shard_map/reduce_scatter | solution.py:324
  518.9 295.0 %reduce-scatter.13.cloned.1.call-start = ((), (), s32[]{:S(2)}) async-start(), calls=%async_computation.12 | async-start | bytes 81920 | tf_op jit(solution)/shard_map/reduce_scatter | solution.py:327
  519.7 297.5 %reduce-scatter.11.cloned.1.call-start = ((), (), s32[]{:S(2)}) async-start(), calls=%async_computation.11 | async-start | bytes 81920 | tf_op jit(solution)/shard_map/reduce_scatter | solution.py:326
  520.0 267.6 %copy-start.77 = (bf16[256]{0:T(256)(128)(2,1)S(1)}, bf16[256]{0:T(256)(128)(2,1)}, u32[]{:S(2)}) copy-start(bf16[256]{0:T(256)(128)(2,1)} %get-tuple-element.412) | copy-start | bytes 1540
  520.0 267.6 %copy-start.6 = (f32[2048,256]{0,1:T(8,128)S(1)}, f32[2048,256]{0,1:T(8,128)}, u32[]{:S(2)}) copy-start(f32[2048,256]{0,1:T(8,128)} %copy-done.4) | copy-start | bytes 6291460
  520.0 267.6 %copy-start.24 = (bf16[512,256]{1,0:T(8,128)(2,1)S(1)}, bf16[512,256]{1,0:T(8,128)(2,1)}, u32[]{:S(2)}) copy-start(bf16[512,256]{1,0:T(8,128)(2,1)} %all_gather.70) | copy-start | bytes 786436
  523.9 379.4 %all-reduce.24.cloned.1.call-start = ((), (), s32[]{:S(2)}) async-start(), calls=%async_computation.18 | async-start | bytes 8650752 | tf_op jit(solution)/shard_map/psum | solution.py:362
  (63 other events, 219.4 us)
Sparse Core Ops, SparseCore 0:
  9.7 140.0 all-gather.3
  151.9 26.3 all-gather.5
  274.8 19.6 reduce-scatter.18
  297.3 19.8 reduce-scatter.20
  319.4 19.9 reduce-scatter.22
  483.6 22.5 reduce-scatter.16
  509.2 43.1 reduce-scatter.14
  554.7 219.6 reduce-scatter.8
  777.2 19.9 reduce-scatter.12
  800.0 17.1 reduce-scatter.10
  821.0 82.2 all-reduce.23
